TPU v7x, 256 devices: a whole 4x4x8 slice. The times are simulated.
256 devices in a mesh: ctx: 32 (over x, z), head: 8 (over y, core).
Axes of the slice: x: 4, y: 4, z: 8, core: 2. Of those that a mesh axis runs over, the one named last changes fastest.
Arguments:
- queries: bfloat16 [65536, 4096], P('ctx', 'head'), may hold values from -28 to 28
- keys: bfloat16 [65536, 1024], P('ctx', 'head'), may hold values from -13 to 13
- values: bfloat16 [65536, 1024], P('ctx', 'head'), may hold values from -6 to 6
- vertical: int32 [8, 16], P('head'), may hold values from 0 to 1023, as said below
- slash: int32 [8, 8], P('head'), may hold values from 0 to 63, as said below
Outputs:
- attention: bfloat16 [65536, 4096], P(('ctx', 'head'))
Inputs may be any that keep to these rules, and one draw needn't show every extreme that they name: `vertical`: each row lists 16 different blocks; at most 4 of one row lie within one index of ctx (2048 tokens), and exactly 4 do in some index. `slash`: each row lists 8 different offsets, 0 and 2 * 32 - 1 among them.
All inputs are finite; a program needn't handle non-finite values.
Results may differ from a plain program's by a relative error of at most 0.0043.
Values may be sent and summed in bfloat16 or wider, within the bound.
A program may use at most 64 MiB of HBM per device.

v0:
```python
import math

import jax
import jax.numpy as jnp
from jax import lax
from jax.sharding import PartitionSpec as P

HD = 128
BLK = 64
NV = 16
NS = 8
MOWN = 4
LOOK = 2


def shifted(array, axis, by):
    count = lax.axis_size(axis)
    pairs = [(i, i + by) for i in range(count) if 0 <= i + by < count]
    return lax.ppermute(array, axis, pairs)


def local(queries, keys, values, vertical, slash):
    shard_count = lax.axis_size("ctx")
    shard_index = lax.axis_index("ctx")
    tok_rows = queries.shape[0]
    kv_local = keys.shape[1] // HD
    group_heads = queries.shape[1] // (kv_local * HD)
    blocks_dev = tok_rows // BLK
    score_scale = 1.0 / math.sqrt(HD)
    offsets = jnp.arange(BLK, dtype=jnp.int32)
    key_value = jnp.stack([keys, values])
    pieces = [key_value]
    current = key_value
    for distance in range(LOOK):
        current = shifted(current, "ctx", 1)
        pieces = [current] + pieces
    window = jnp.concatenate(pieces, axis=1).reshape(2, (LOOK + 1) * blocks_dev, BLK, kv_local, HD)
    owners = vertical // blocks_dev
    local_block = vertical % blocks_dev
    owned_here = owners == shard_index
    local_pairs = key_value.reshape(2, blocks_dev, BLK, kv_local, HD)
    block_hot = (local_block[:, :, None] == jnp.arange(blocks_dev, dtype=jnp.int32)).astype(
        jnp.bfloat16
    )
    list_index = jnp.arange(NV, dtype=jnp.int32)
    same_owner = owners[:, :, None] == owners[:, None, :]
    earlier = list_index[None, :] < list_index[:, None]
    slot_rank = jnp.sum((same_owner & earlier[None]).astype(jnp.int32), axis=2)
    slot_hot = (
        (slot_rank[:, :, None] == jnp.arange(MOWN, dtype=jnp.int32)) & owned_here[:, :, None]
    ).astype(jnp.bfloat16)
    slot_picker = jnp.einsum(
        "jnm,jnb->jmb", slot_hot, block_hot, preferred_element_type=jnp.float32
    ).astype(jnp.bfloat16)
    slots = jnp.einsum(
        "jmb,xbtjd->xjmtd", slot_picker, local_pairs, preferred_element_type=jnp.float32
    ).astype(jnp.bfloat16)
    gathered = lax.all_gather(slots, "ctx", axis=2, tiled=True)
    slot_index = owners * MOWN + slot_rank
    chooser = (slot_index[:, :, None] == jnp.arange(shard_count * MOWN, dtype=jnp.int32)).astype(
        jnp.bfloat16
    )
    vert_pairs = jnp.einsum(
        "jns,xjstd->xjntd", chooser, gathered, preferred_element_type=jnp.float32
    ).astype(jnp.bfloat16)
    vert_keys = vert_pairs[0].reshape(kv_local, NV * BLK, HD)
    vert_values = vert_pairs[1].reshape(kv_local, NV * BLK, HD)
    vert_pos = (vertical[:, :, None] * BLK + offsets).reshape(kv_local, NV * BLK)
    query_blocks = queries.reshape(blocks_dev, BLK, kv_local, group_heads, HD)

    def take_head(window_head, indices):
        return jnp.take(window_head, indices.reshape(-1), axis=1).reshape(2, NS, 2, BLK, HD)

    def attend_group(group_index):
        group_blocks = group_index * 2 + jnp.arange(2, dtype=jnp.int32)
        window_index = group_blocks[None, None, :] + LOOK * blocks_dev - slash[:, :, None]
        slash_pairs = jax.vmap(take_head, in_axes=(3, 0))(window, window_index)
        slash_keys = slash_pairs[:, 0]
        slash_values = slash_pairs[:, 1]
        query_group = lax.dynamic_slice_in_dim(query_blocks, group_index * 2, 2, 0)
        global_blocks = shard_index * blocks_dev + group_blocks
        query_pos = global_blocks[:, None] * BLK + offsets[None, :]
        vert_scores = (
            jnp.einsum(
                "grjhd,jkd->jhgrk", query_group, vert_keys, preferred_element_type=jnp.float32
            )
            * score_scale
        )
        vert_allowed = vert_pos[:, None, None, :] <= query_pos[None, :, :, None]
        vert_scores = jnp.where(vert_allowed[:, None], vert_scores, -1e30)
        slash_blocks = global_blocks[None, None, :] - slash[:, :, None]
        in_vertical = jnp.any(slash_blocks[:, :, :, None] == vertical[:, None, None, :], axis=3)
        slash_valid = jnp.transpose((slash_blocks >= 0) & jnp.logical_not(in_vertical), (0, 2, 1))
        slash_pos = jnp.transpose(slash_blocks, (0, 2, 1))[:, :, :, None] * BLK + offsets
        slash_allowed = slash_valid[:, :, None, :, None] & (
            slash_pos[:, :, None, :, :] <= query_pos[None, :, :, None, None]
        )
        slash_scores = (
            jnp.einsum(
                "grjhd,jngtd->jhgrnt", query_group, slash_keys, preferred_element_type=jnp.float32
            )
            * score_scale
        )
        slash_scores = jnp.where(slash_allowed[:, None], slash_scores, -1e30)
        row_max = jnp.maximum(jnp.max(vert_scores, axis=4), jnp.max(slash_scores, axis=(4, 5)))
        vert_weights = jnp.exp(vert_scores - row_max[..., None])
        slash_weights = jnp.exp(slash_scores - row_max[..., None, None])
        denominator = jnp.sum(vert_weights, axis=4) + jnp.sum(slash_weights, axis=(4, 5))
        weighted = jnp.einsum(
            "jhgrk,jkd->grjhd",
            vert_weights.astype(jnp.bfloat16),
            vert_values,
            preferred_element_type=jnp.float32,
        )
        weighted = weighted + jnp.einsum(
            "jhgrnt,jngtd->grjhd",
            slash_weights.astype(jnp.bfloat16),
            slash_values,
            preferred_element_type=jnp.float32,
        )
        return (weighted / jnp.transpose(denominator, (2, 3, 0, 1))[..., None]).astype(jnp.bfloat16)

    attended = lax.map(attend_group, jnp.arange(blocks_dev // 2, dtype=jnp.int32))
    attended = attended.reshape(tok_rows, kv_local * group_heads * HD)
    return lax.all_to_all(attended, "head", split_axis=0, concat_axis=1, tiled=True)


def solution(mesh):
    in_specs = (
        P("ctx", "head"),
        P("ctx", "head"),
        P("ctx", "head"),
        P("head", None),
        P("head", None),
    )
    out_specs = P(("ctx", "head"), None)
    return jax.shard_map(local, mesh=mesh, in_specs=in_specs, out_specs=out_specs, check_vma=False)
```

profile of v0, /device:TPU:0, one launch (start us, length us, event | category | flops | bytes accessed | tf_op | source)
XLA Modules:
  0.0 314.4 jit_solution(12594161390055221487)
XLA Ops:
  8.1 2.2 copy.78
  10.3 2.2 copy.79
  12.5 1.8 fusion.35
  15.1 3.1 collective-permute-start
  18.2 23.9 %collective-permute-done = bf16[2,2048,128]{2,1,0:T(8,128)(2,1)} collective-permute-done((bf16[2,2048,128]{2,1,0:T(8,128)(2,1)S(1)}, bf16[2,2048,128]{2,1,0:T(8,128)(2,1)}, u32[]{:S(2)}, u32[]{:S(2)}) %collective-permute-start) | collective-permute-done | bytes 1048608 | tf_op jit(solution)/shard_map/ppermute | solution.py:19
  42.1 5.5 %collective-permute-start.1 = (bf16[2,2048,128]{2,1,0:T(8,128)(2,1)}, bf16[2,2048,128]{2,1,0:T(8,128)(2,1)}, u32[]{:S(2)}, u32[]{:S(2)}) collective-permute-start(bf16[2,2048,128]{2,1,0:T(8,128)(2,1)} %collective-permute-done), channel_id=1, source_target_pairs={{0,8},{8,16},{16,24},{24,32},{32,40},{40,48},{48,56},{56,64},{64,7... | collective-permute-start | bytes 3145736 | tf_op jit(solution)/shard_map/ppermute | solution.py:19
  47.5 2.1 reshape.913
  49.6 23.0 %collective-permute-done.1 = bf16[2,2048,128]{2,1,0:T(8,128)(2,1)} collective-permute-done((bf16[2,2048,128]{2,1,0:T(8,128)(2,1)}, bf16[2,2048,128]{2,1,0:T(8,128)(2,1)}, u32[]{:S(2)}, u32[]{:S(2)}) %collective-permute-start.1) | collective-permute-done | bytes 1048608 | tf_op jit(solution)/shard_map/ppermute | solution.py:19
  72.6 9.9 %maximum_maximum_fusion = bf16[2,6144,128]{2,1,0:T(8,128)(2,1)} fusion(bf16[1,2048,128]{2,1,0:T(8,128)(2,1)S(1)} %bitcast.217, bf16[1,2048,128]{2,1,0:T(8,128)(2,1)S(1)} %bitcast.220, bf16[2,2048,128]{2,1,0:T(8,128)(2,1)} %collective-permute-done, bf16[2,2048,128]{2,1,0:T(8,128)(2,1)} %collective-permute-done.1), kind=kLoop, calls=%fused_computation.56 | loop fusion | flops 12582912 | bytes 6291456 | tf_op jit(solution)/shard_map/concatenate | solution.py:37
  82.5 17.2 %all-gather.2.cloned.1.call-done = bf16[2,1,128,64,128]{4,3,1,0,2:T(8,128)(2,1)} async-done(((bf16[2,1,4,64,128]{4,3,1,0,2:T(8,128)(2,1)}), bf16[2,1,128,64,128]{4,3,1,0,2:T(8,128)(2,1)}) %all-gather.2.cloned.1.call-update) | async-done | bytes 4194320 | tf_op jit(solution)/shard_map/all_gather | solution.py:58
  99.7 4.5 %fusion.32 = bf16[2,1,16,64,128]{4,2,3,0,1:T(8,128)(2,1)S(1)} fusion(bf16[2,1,128,64,128]{4,3,1,0,2:T(8,128)(2,1)} %all-gather.2.cloned.1.call-done, s32[16]{0:T(128)S(1)} %fusion.57), kind=kOutput, calls=%fused_computation.58 | convolution fusion | flops 67373056 | bytes 4718656 | tf_op jit(solution)/shard_map/jns,xjstd->xjntd/dot_general | solution.py:63
  104.9 162.6 %while.14 = (s32[]{:T(128)}, bf16[16,2,64,1,4,128]{5,4,2,1,0,3:T(4,128)(2,1)}, s32[]{:T(128)}, s32[16]{0:T(128)S(1)}, bf16[32,64,1,4,128]{4,3,1,0,2:T(4,128)(2,1...) while((s32[]{:T(128)}, ...), condition=%wide.region_7.8_spmd.clone.clone, body=%wide.region_1.7_spmd.clone.clone.sunk | while | flops 408094720 | bytes 15069147 | solution.py:123
  107.3 2.5 gather_fusion
  110.1 1.0 constant_dynamic-slice_fusion.2
  117.5 2.5 gather_fusion
  120.3 1.0 constant_dynamic-slice_fusion.2
  127.7 2.5 gather_fusion
  130.4 1.0 constant_dynamic-slice_fusion.2
  137.8 2.5 gather_fusion
  140.6 1.0 constant_dynamic-slice_fusion.2
  148.0 2.5 gather_fusion
  150.7 1.0 constant_dynamic-slice_fusion.2
  158.2 2.5 gather_fusion
  160.9 1.0 constant_dynamic-slice_fusion.2
  168.3 2.5 gather_fusion
  171.1 1.0 constant_dynamic-slice_fusion.2
  178.5 2.5 gather_fusion
  181.2 1.0 constant_dynamic-slice_fusion.2
  188.6 2.5 gather_fusion
  191.4 1.0 constant_dynamic-slice_fusion.2
  198.8 2.5 gather_fusion
  201.6 1.0 constant_dynamic-slice_fusion.2
  209.0 2.5 gather_fusion
  211.7 1.0 constant_dynamic-slice_fusion.2
  219.1 2.5 gather_fusion
  221.9 1.0 constant_dynamic-slice_fusion.2
  229.3 2.5 gather_fusion
  232.1 1.0 constant_dynamic-slice_fusion.2
  239.5 2.5 gather_fusion
  242.2 1.0 constant_dynamic-slice_fusion.2
  249.6 2.5 gather_fusion
  252.4 1.0 constant_dynamic-slice_fusion.2
  259.8 2.5 gather_fusion
  262.6 1.0 constant_dynamic-slice_fusion.2
  267.6 2.7 all_to_all.14
  270.3 31.5 %all_to_all.19 = bf16[8,256,512]{2,1,0:T(8,128)(2,1)} all-to-all(bf16[8,256,512]{2,1,0:T(8,128)(2,1)S(1)} %all_to_all.14), channel_id=1, replica_groups=mesh['ctx'=32,'head'=8] {'head'}, dimensions={0} | all-to-all | bytes 4194304 | tf_op jit(solution)/shard_map/all_to_all | solution.py:125
  301.8 2.8 copy.86
  304.7 2.9 copy.87
  (519 shorter events, 97.6 us)
Async XLA Ops:
  6.5 93.2 %all-gather.2.cloned.1.call-start = ((), (), s32[]{:S(2)}) async-start(), calls=%async_computation.1 | async-start | bytes 4325376 | tf_op jit(solution)/shard_map/all_gather | solution.py:58
  8.0 6.9 %copy-start = (bf16[2048,128]{1,0:T(8,128)(2,1)S(1)}, bf16[2048,128]{1,0:T(8,128)(2,1)}, u32[]{:S(2)}) copy-start(bf16[2048,128]{1,0:T(8,128)(2,1)} %param.9) | copy-start | bytes 1572868
  8.1 6.9 %copy-start.1 = (bf16[2048,128]{1,0:T(8,128)(2,1)S(1)}, bf16[2048,128]{1,0:T(8,128)(2,1)}, u32[]{:S(2)}) copy-start(bf16[2048,128]{1,0:T(8,128)(2,1)} %param.8) | copy-start | bytes 1572868
  12.5 35.1 %copy-start.2 = (bf16[2048,512]{1,0:T(8,128)(2,1)S(1)}, bf16[2048,512]{1,0:T(8,128)(2,1)}, u32[]{:S(2)}) copy-start(bf16[2048,512]{1,0:T(8,128)(2,1)} %param.7) | copy-start | bytes 6291460
  15.1 27.0 %collective-permute-start = (bf16[2,2048,128]{2,1,0:T(8,128)(2,1)S(1)}, bf16[2,2048,128]{2,1,0:T(8,128)(2,1)}, u32[]{:S(2)}, u32[]{:S(2)}) collective-permute-start(bf16[2,2048,128]{2,1,0:T(8,128)(2,1)S(1)} %pad_maximum_fusion), channel_id=1, source_target_pairs={{0,8},{8,16},{16,24},{24,32},{32,40},{40,48},{48,56},{56,64},{64,7... | collective-permute-start | bytes 3145736 | tf_op jit(solution)/shard_map/ppermute | solution.py:19
  42.1 30.5 %collective-permute-start.1 = (bf16[2,2048,128]{2,1,0:T(8,128)(2,1)}, bf16[2,2048,128]{2,1,0:T(8,128)(2,1)}, u32[]{:S(2)}, u32[]{:S(2)}) collective-permute-start(bf16[2,2048,128]{2,1,0:T(8,128)(2,1)} %collective-permute-done), channel_id=1, source_target_pairs={{0,8},{8,16},{16,24},{24,32},{32,40},{40,48},{48,56},{56,64},{64,7... | collective-permute-start | bytes 3145736 | tf_op jit(solution)/shard_map/ppermute | solution.py:19
  104.3 0.7 copy-start.3
  104.3 0.7 copy-start.4
Sparse Core Ops, SparseCore 0:
  15.1 84.5 all-gather.1
where the time goes:
time: 319 us; the launch traced here: 314 us
  local copies, waits for them, and re-layouts  99.9 us (31%)
  waiting for transfers between devices  64.1 us (20%)
  other arithmetic  46.3 us (15%)
  matrix products  38.5 us (12%)
  blocking collectives  31.5 us (10%)
  between operations  13.5 us (4%)
  loops' own time  12.1 us (4%)
  starting transfers between devices  8.55 us (3%)
    ppermute x2, waiting for transfers between devices, shifted(): return lax.ppermute(array, axis, pairs)  46.9 us
    gather x32, local copies, waits for them, and re-layouts, take_head(): jnp.take(window_head, indices.reshape(-1), axis=1)  40.8 us
    all_to_all x1, blocking collectives, local(): lax.all_to_all(attended, 'head', split_axis=0, concat_axis=1, tiled=True)  31.5 us
    all_gather x1, waiting for transfers between devices, local(): gathered = lax.all_gather(slots, 'ctx', axis=2, tiled=True)  17.2 us
    dynamic_slice x16, local copies, waits for them, and re-layouts, attend_group(): query_group = lax.dynamic_slice_in_dim(query_blocks, group_index * 2, 2, 0)  15.3 us
    dynamic_update_slice x16, local copies, waits for them, and re-layouts, local(): lax.map(attend_group, jnp.arange(blocks_dev // 2, dtype=jnp.int32))  12.2 us
    another operation x1, loops' own time, local(): lax.map(attend_group, jnp.arange(blocks_dev // 2, dtype=jnp.int32))  12.1 us
    dynamic_slice x16, local copies, waits for them, and re-layouts, local(): lax.map(attend_group, jnp.arange(blocks_dev // 2, dtype=jnp.int32))  10.4 us
  transfers between devices with their start and end apart: 3, of which 3 were waited for; matrix products, arithmetic and copies ran while one was open for 4% of the time, Pallas kernels for 0%

commit v1 on v0

v1 whole, which is shorter than its diff:
```python
import functools
import math

import jax
import jax.numpy as jnp
from jax import lax
from jax.experimental import pallas as pl
from jax.experimental.pallas import tpu as pltpu
from jax.sharding import PartitionSpec as P

HD = 128
BLK = 64
LOOK = 2
NX = 4
NEG = -1e30
MESH = pl.DeviceIdType.MESH
F32 = jnp.float32
BF16 = jnp.bfloat16


def kernel(cfg, vert, slash, q_ref, k_ref, v_ref, out_ref, win_k, win_v, land1, land2, ext, rx, sx, rz, vall, bias, stage,
           own_send, own_recv, fwd_send, fwd_recv, xs_send, xs_recv, zs_send, zs_recv, zg_send, zg_recv, xg_send, xg_recv,
           out_send, out_recv, loc_sem):
    nx, nz, nh, nv, ns, nb, hq = cfg
    nctx = nx * nz
    bpc = nb // nh
    per = nv // nx
    vk = nv * BLK
    sk = ns * BLK
    ctx = lax.axis_index("ctx")
    me = lax.axis_index("head")
    x = ctx // nz
    z = ctx % nz
    nxt = (ctx + 1) % nctx
    prv = (ctx + nctx - 1) % nctx

    def xpeer(d):
        return ((x + d) % nx) * nz + z

    def zpeer(d):
        return x * nz + (z + d) % nz

    barrier = pltpu.get_barrier_semaphore()

    def greet(c, h):
        pl.semaphore_signal(barrier, inc=1, device_id={"ctx": c, "head": h}, device_id_type=MESH)

    greet(nxt, me)
    greet(prv, me)
    for d in range(1, nx):
        greet(xpeer(d), me)
    for d in range(1, nz):
        greet(zpeer(d), me)
    for d in range(1, nh):
        greet(ctx, (me + d) % nh)
    pl.semaphore_wait(barrier, 2 + (nx - 1) + (nz - 1) + (nh - 1))

    def remote(src, dst, ssem, rsem, c, h):
        return pltpu.make_async_remote_copy(src_ref=src, dst_ref=dst, send_sem=ssem, recv_sem=rsem,
                                            device_id={"ctx": c, "head": h}, device_id_type=MESH)

    def own_copy(k, part):
        ref = k_ref if part == 0 else v_ref
        return remote(ref.at[pl.ds(k * bpc, bpc)], land1.at[k, part], own_send.at[k, part],
                      own_recv.at[k, part], nxt, me)

    def fwd_copy(k):
        return remote(land1.at[k], land2.at[k], fwd_send.at[k], fwd_recv.at[k], nxt, me)

    def send_own(k):
        own_copy(k, 0).start()
        own_copy(k, 1).start()

    def take_own(k):
        own_copy(k, 0).wait_recv()
        own_copy(k, 1).wait_recv()
        fwd_copy(k).start()
        for b in range(bpc):
            win_k[nb + k * bpc + b] = land1[k, 0, b]
            win_v[nb + k * bpc + b] = land1[k, 1, b]

    own_left = [nh - 1 - k for k in range(nh)]
    take_left = list(own_left)

    def send_some(count):
        for _ in range(min(count, len(own_left))):
            send_own(own_left.pop(0))

    def take_some(count):
        for _ in range(min(count, len(take_left))):
            take_own(take_left.pop(0))

    send_some(3)

    for part in range(nx):
        for slot in range(per):
            rel = vert[0, part * per + slot] - ctx * nb
            mine = (rel >= 0) & (rel < nb)
            at = jnp.minimum(jnp.maximum(rel, 0), nb - 1)
            ext[part, slot] = jnp.where(mine, k_ref[at], jnp.zeros((BLK, HD), BF16))
            ext[part, per + slot] = jnp.where(mine, v_ref[at], jnp.zeros((BLK, HD), BF16))

    def xs_copy(d):
        return remote(ext.at[(x + d) % nx], rx.at[d - 1], xs_send.at[d - 1], xs_recv.at[d - 1], xpeer(d), me)

    def zs_copy(d):
        return remote(sx.at[(z + d) % nz], rz.at[d - 1], zs_send.at[d - 1], zs_recv.at[d - 1], zpeer(d), me)

    def zg_copy(d):
        return remote(vall.at[x, z], vall.at[x, z], zg_send.at[d - 1], zg_recv.at[d - 1], zpeer(d), me)

    def zg_arrival(d):
        src = (z + nz - d) % nz
        return remote(vall.at[x, src], vall.at[x, src], zg_send.at[d - 1], zg_recv.at[d - 1], zpeer(d), me)

    def xg_copy(d):
        return remote(vall.at[x], vall.at[x], xg_send.at[d - 1], xg_recv.at[d - 1], xpeer(d), me)

    def xg_arrival(d):
        src = (x + nx - d) % nx
        return remote(vall.at[src], vall.at[src], xg_send.at[d - 1], xg_recv.at[d - 1], xpeer(d), me)

    for d in range(1, nx):
        xs_copy(d).start()

    def copy_own(b, carry):
        win_k[LOOK * nb + b] = k_ref[b]
        win_v[LOOK * nb + b] = v_ref[b]
        return carry

    lax.fori_loop(0, nb, copy_own, 0)
    block = ctx * nb + lax.broadcasted_iota(jnp.int32, (nb, vk), 0)
    lane = lax.broadcasted_iota(jnp.int32, (nb, vk), 1) // BLK
    listed = jnp.zeros((nb, vk), jnp.int32)
    for n in range(nv):
        listed = jnp.where(lane == n, vert[0, n], listed)
    bias[:, 0:vk] = jnp.where(listed < block, 0.0, NEG)

    def offset(n):
        first = slash[0, 0]
        own = slash[0, n]
        return jnp.int32(0) if n == 0 else jnp.where(own == 0, first, own)

    reach = jnp.zeros((nb, sk), jnp.int32)
    for n in range(ns):
        reach = jnp.where(lane[:, 0:sk] == n, offset(n), reach)
    target = block[:, 0:sk] - reach
    good = target >= 0
    for n in range(nv):
        good = good & (target != vert[0, n])
    good = good | (lane[:, 0:sk] == 0)
    bias[:, vk:vk + sk] = jnp.where(good, 0.0, NEG)

    for d in range(1, nx):
        xs_copy(d).wait_recv()
    sx[...] = ext[x]
    for d in range(1, nx):
        sx[...] = sx[...] + rx[d - 1]
    for d in range(1, nz):
        zs_copy(d).start()
    send_some(2)
    take_some(1)
    for d in range(1, nz):
        zs_copy(d).wait_recv()
    piece = sx[z]
    for d in range(1, nz):
        piece = piece + rz[d - 1]
    vall[x, z] = piece
    for d in range(1, nz):
        zg_copy(d).start()
    send_some(2)
    take_some(2)
    for d in range(1, nz):
        zg_arrival(d).wait_recv()
    for d in range(1, nx):
        xg_copy(d).start()
    send_some(nh)
    take_some(nh)
    for d in range(1, nx):
        xg_arrival(d).wait_recv()

    factor = math.log2(math.e) / math.sqrt(HD)
    nt = (((1,), (1,)), ((), ()))
    cols = hq * HD
    qrows = hq * BLK
    tri_t = lax.broadcasted_iota(jnp.int32, (qrows, 2 * BLK), 0) % BLK
    tri_u = lax.broadcasted_iota(jnp.int32, (qrows, 2 * BLK), 1)
    causal = jnp.where((tri_u > tri_t) & (tri_u < BLK), NEG, 0.0)
    group = 256 // BLK

    def attend(r, to):
        q = q_ref[pl.ds(pl.multiple_of(r * BLK, BLK), BLK), :]
        qs = jnp.concatenate([q[:, h * HD:(h + 1) * HD] for h in range(hq)], axis=0)
        scores = []
        vals = []
        for part in range(nx):
            kk = vall[part, 0:per].reshape(per * BLK, HD)
            s = lax.dot_general(qs, kk, nt, preferred_element_type=F32)
            scores.append(s + bias[pl.ds(r, 1), part * per * BLK:(part + 1) * per * BLK])
            vals.append(lambda part=part: vall[part, per:2 * per].reshape(per * BLK, HD))
        for g in range(0, ns, group):
            at = [r + LOOK * nb - offset(n) for n in range(g, g + group)]
            kk = jnp.concatenate([win_k[a] for a in at], axis=0)
            s = lax.dot_general(qs, kk, nt, preferred_element_type=F32)
            s = s + bias[pl.ds(r, 1), vk + g * BLK:vk + (g + group) * BLK]
            if g == 0:
                s = jnp.concatenate([s[:, 0:2 * BLK] + causal, s[:, 2 * BLK:]], axis=1)
            scores.append(s)
            vals.append(lambda at=at: jnp.concatenate([win_v[a] for a in at], axis=0))
        top = jnp.max(scores[0], axis=1, keepdims=True)
        for s in scores[1:]:
            top = jnp.maximum(top, jnp.max(s, axis=1, keepdims=True))
        top = top * factor
        total = jnp.zeros((qrows, 1), F32)
        acc = jnp.zeros((qrows, HD), F32)
        for s, val in zip(scores, vals):
            w = jnp.exp2(s * factor - top)
            total = total + jnp.sum(w, axis=1, keepdims=True)
            acc = acc + jnp.dot(w.astype(BF16), val(), preferred_element_type=F32)
        o = (acc / total).astype(BF16)
        for h in range(hq):
            stage[to, pl.ds(pl.multiple_of((r % bpc) * BLK, BLK), BLK), h * HD:(h + 1) * HD] = o[h * BLK:(h + 1) * BLK]

    def out_copy(ch):
        return remote(stage.at[ch], out_ref.at[:, pl.ds(pl.multiple_of(me * cols, cols), cols)], out_send.at[ch],
                      out_recv.at[me], ctx, ch)

    def out_arrival(src):
        return remote(stage.at[src], out_ref.at[:, pl.ds(pl.multiple_of(src * cols, cols), cols)], out_send.at[src],
                      out_recv.at[src], ctx, src)

    def out_local():
        return pltpu.make_async_copy(stage.at[me], out_ref.at[:, pl.ds(pl.multiple_of(me * cols, cols), cols)], loc_sem)

    def chunk(step, carry):
        ch = nh - 1 - step
        fwd_copy(ch).wait_recv()

        def fill(b, c):
            win_k[ch * bpc + b] = land2[ch, 0, b]
            win_v[ch * bpc + b] = land2[ch, 1, b]
            return c

        lax.fori_loop(0, bpc, fill, 0)

        def one(j, c):
            attend(ch * bpc + bpc - 1 - j, ch)
            return c

        lax.fori_loop(0, bpc, one, 0)

        @pl.when(ch != me)
        def _():
            out_copy(ch).start()

        @pl.when(ch == me)
        def _():
            out_local().start()

        return carry

    lax.fori_loop(0, nh, chunk, 0)

    for k in range(nh):
        own_copy(k, 0).wait_send()
        own_copy(k, 1).wait_send()
        fwd_copy(k).wait_send()
    for d in range(1, nx):
        xs_copy(d).wait_send()
        xg_copy(d).wait_send()
    for d in range(1, nz):
        zs_copy(d).wait_send()
        zg_copy(d).wait_send()
    for ch in range(nh):
        @pl.when(ch != me)
        def _(ch=ch):
            out_copy(ch).wait_send()
            out_arrival(ch).wait_recv()
    out_local().wait()


def solution(mesh, nx=NX):
    nh = mesh.shape["head"]
    nctx = mesh.shape["ctx"]
    nz = nctx // nx

    def local(queries, keys, values, vertical, slash):
        tok, qcols = queries.shape
        hq = qcols // HD
        nb = tok // BLK
        nv = vertical.shape[1]
        ns = slash.shape[1]
        assert 2 * nv == nx * nz
        cfg = (nx, nz, nh, nv, ns, nb, hq)
        rows = tok // nh
        per = nv // nx
        dma = pltpu.SemaphoreType.DMA
        vmem = pl.BlockSpec(memory_space=pltpu.VMEM)
        smem = pl.BlockSpec(memory_space=pltpu.SMEM)
        return pl.pallas_call(
            functools.partial(kernel, cfg),
            out_shape=jax.ShapeDtypeStruct((rows, nh * qcols), BF16),
            in_specs=[smem, smem, vmem, vmem, vmem],
            out_specs=pl.BlockSpec(memory_space=pl.ANY),
            scratch_shapes=[
                pltpu.VMEM(((LOOK + 1) * nb, BLK, HD), BF16),
                pltpu.VMEM(((LOOK + 1) * nb, BLK, HD), BF16),
                pltpu.VMEM((nh, 2, nb // nh, BLK, HD), BF16),
                pltpu.VMEM((nh, 2, nb // nh, BLK, HD), BF16),
                pltpu.VMEM((nx, nz, BLK, HD), BF16),
                pltpu.VMEM((nx - 1, nz, BLK, HD), BF16),
                pltpu.VMEM((nz, BLK, HD), BF16),
                pltpu.VMEM((nz - 1, BLK, HD), BF16),
                pltpu.VMEM((nx, nz, BLK, HD), BF16),
                pltpu.VMEM((nb, (nv + ns) * BLK), F32),
                pltpu.VMEM((nh, rows, qcols), BF16),
                dma((nh, 2)), dma((nh, 2)), dma((nh,)), dma((nh,)),
                dma((nx - 1,)), dma((nx - 1,)), dma((nz - 1,)), dma((nz - 1,)),
                dma((nz - 1,)), dma((nz - 1,)), dma((nx - 1,)), dma((nx - 1,)),
                dma((nh,)), dma((nh,)), dma(()),
            ],
            compiler_params=pltpu.CompilerParams(collective_id=0, has_side_effects=True, vmem_limit_bytes=56 * 1024 * 1024),
        )(vertical, slash, queries, keys.reshape(nb, BLK, HD), values.reshape(nb, BLK, HD))

    in_specs = (P("ctx", "head"), P("ctx", "head"), P("ctx", "head"), P("head", None), P("head", None))
    return jax.shard_map(local, mesh=mesh, in_specs=in_specs, out_specs=P(("ctx", "head"), None), check_vma=False)
```

time: 319 us -> 132 us (0.41); the launches traced: 314 us -> 131 us
  Pallas kernels: 0 us -> 128 us
  local copies, waits for them, and re-layouts: 99.9 us -> 3.13 us
  waiting for transfers between devices: 64.1 us -> 0 us
  other arithmetic: 46.3 us -> 0 us
  matrix products: 38.5 us -> 0 us
  blocking collectives: 31.5 us -> 0 us
  between operations: 13.5 us -> 0.01 us
  loops' own time: 12.1 us -> 0 us
  starting transfers between devices: 8.55 us -> 0 us
    pallas_call x0 -> x1, Pallas kernels: none -> 128 us  [local(): pl.pallas_call(functools.partial(kernel, cfg), out_shape=jax.ShapeDtypeSt...]
    ppermute x2 -> x0, waiting for transfers between devices: 46.9 us -> none  [shifted(): return lax.ppermute(array, axis, pairs)]
    gather x32 -> x0, local copies, waits for them, and re-layouts: 40.8 us -> none  [take_head(): jnp.take(window_head, indices.reshape(-1), axis=1)]
    dot_general x66 -> x0, matrix products: 38.5 us -> none  [the longest x16 9.32 us: attend_group(): jnp.einsum('grjhd,jkd->jhgrk', query_group, vert_keys, preferred_element_...]
    all_to_all x1 -> x0, blocking collectives: 31.5 us -> none  [local(): lax.all_to_all(attended, 'head', split_axis=0, concat_axis=1, tiled=True)]
    dynamic_slice x32 -> x0, local copies, waits for them, and re-layouts: 25.7 us -> none  [the longest x16 15.3 us: attend_group(): query_group = lax.dynamic_slice_in_dim(query_blocks, group_index * 2, 2, 0)]
    all_gather x1 -> x0, waiting for transfers between devices: 17.2 us -> none  [local(): gathered = lax.all_gather(slots, 'ctx', axis=2, tiled=True)]
    reduce_sum x33 -> x0, other arithmetic: 15 us -> none  [the longest x16 7.77 us: attend_group(): jnp.sum(vert_weights, axis=4) + jnp.sum(slash_weights, axis=(4, 5))]
  transfers between devices with their start and end apart: 3 -> 0, of which waited for: 3 -> 0; matrix products, arithmetic and copies ran while one was open for 4% -> 0% of each run, Pallas kernels for 0% -> 0%
where the time goes in v1:
time: 132 us; the launch traced here: 131 us
  Pallas kernels  128 us (97%)
  local copies, waits for them, and re-layouts  3.13 us (2%)
    pallas_call x1, Pallas kernels, local(): pl.pallas_call(functools.partial(kernel, cfg), out_shape=jax.ShapeDtypeSt...  128 us
    unnamed x1, local copies, waits for them, and re-layouts  3.13 us

profile of v1, /device:TPU:0, one launch (start us, length us, event | category | flops | bytes accessed | tf_op | source)
XLA Modules:
  0.0 131.4 jit_solution(10020537919139546377)
XLA Ops:
  0.0 128.3 %shard_map.55 = bf16[256,4096]{1,0:T(8,128)(2,1)} custom-call(s32[1,16]{1,0:T(1,128)} %vert.1, s32[1,8]{1,0:T(1,128)} %slash.1, bf16[2048,512]{1,0:T(8,128)(2,1)} %q_ref.1, bf16[32,64,128]{2,1,0:T(8,128)(2,1)} %bitcast.2, bf16[32,64,128]{2,1,0:T(8,128)(2,1)} %bitcast.3), custom_call_target="tpu_custom_call" | custom-call | tf_op jit(solution)/shard_map/pallas_call | solution.py:300
  128.3 3.1 %copy.7 = bf16[256,4096]{1,0:T(8,128)(2,1)} copy(bf16[256,4096]{1,0:T(8,128)(2,1)} %shard_map.55) | data formatting | bytes 4194304

commit v2 on v1

v2 whole, which is shorter than its diff:
```python
import functools
import math

import jax
import jax.numpy as jnp
from jax import lax
from jax.experimental import pallas as pl
from jax.experimental.pallas import tpu as pltpu
from jax.sharding import PartitionSpec as P

HD = 128
BLK = 64
LOOK = 2
NX = 4
NEG = -1e30
MESH = pl.DeviceIdType.MESH
F32 = jnp.float32
BF16 = jnp.bfloat16


def kernel(cfg, vert, slash, q_ref, k_ref, v_ref, out_ref, q_buf, v_buf, win_k, win_v, land1, land2, land_a, ext, rx, sx, rz,
           vall, vturn, stage, buf_a, buf_b, tops, shifts, own_send, own_recv, fwd_send, fwd_recv, a_send, a_recv, bc_send, bc_recv, xs_send, xs_recv,
           zs_send, zs_recv, zg_send, zg_recv, xg_send, xg_recv, out_send, out_recv, loc_sem):
    nx, nz, nh, nv, ns, nb, hq = cfg
    nctx = nx * nz
    bpc = nb // nh
    per = nv // nx
    half = (nz - 2) // 2
    own0 = LOOK * nb
    cols = hq * HD
    qrows = hq * BLK
    group = 256 // BLK
    ctx = lax.axis_index("ctx")
    me = lax.axis_index("head")
    x = ctx // nz
    z = ctx % nz
    nxt = (ctx + 1) % nctx
    prv = (ctx + nctx - 1) % nctx

    def xpeer(d):
        return ((x + d) % nx) * nz + z

    def zpeer(d):
        return x * nz + (z + d) % nz

    relay_to = (zpeer(half) + 2) % nctx
    two_back = (ctx + nctx - 2) % nctx
    relay_from = (two_back // nz) * nz + (two_back % nz + nz - half) % nz

    load_k = pltpu.make_async_copy(k_ref, win_k.at[pl.ds(own0, nb)], loc_sem.at[0])
    load_v = pltpu.make_async_copy(v_ref, v_buf, loc_sem.at[1])
    load_q = pltpu.make_async_copy(q_ref, q_buf, loc_sem.at[2])
    load_k.start()
    load_v.start()
    load_q.start()

    barrier = pltpu.get_barrier_semaphore()

    def greet(c, h):
        pl.semaphore_signal(barrier, inc=1, device_id={"ctx": c, "head": h}, device_id_type=MESH)

    for c in (nxt, prv, relay_to, relay_from):
        greet(c, me)
    for d in range(1, nx):
        greet(xpeer(d), me)
    for d in range(1, nz):
        greet(zpeer(d), me)
    for d in range(1, nh):
        greet(ctx, (me + d) % nh)
    pl.semaphore_wait(barrier, 4 + (nx - 1) + (nz - 1) + (nh - 1))

    def remote(src, dst, ssem, rsem, c, h):
        return pltpu.make_async_remote_copy(src_ref=src, dst_ref=dst, send_sem=ssem, recv_sem=rsem,
                                            device_id={"ctx": c, "head": h}, device_id_type=MESH)

    def own_copy(k, part):
        ref = k_ref if part == 0 else v_ref
        return remote(ref.at[pl.ds(k * bpc, bpc)], land1.at[k, part], own_send.at[k, part], own_recv.at[k, part], nxt, me)

    def fwd_copy(k):
        return remote(land1.at[k], land2.at[k], fwd_send.at[k], fwd_recv.at[k], nxt, me)

    def a_copy(part):
        ref = k_ref if part == 0 else v_ref
        return remote(ref.at[pl.ds(0, bpc)], land_a.at[part], a_send.at[part], a_recv.at[part], zpeer(nz - half), me)

    def b_copy():
        return remote(land_a, land2.at[0], bc_send.at[0], bc_recv.at[0], relay_to, me)

    def c_copy():
        return remote(land2.at[0], land1.at[0], bc_send.at[1], bc_recv.at[1], prv, me)

    def send_own(k):
        own_copy(k, 0).start()
        own_copy(k, 1).start()

    def turn(dst, at, one, two):
        dst[at] = jnp.concatenate([one, two], axis=0).T
        dst[at + 1] = jnp.concatenate([two, one], axis=0).T

    def place(land, k, base):
        def pair(p, c):
            b = 2 * p
            at = base + k * bpc + b
            win_k[at] = land[k, 0, b]
            win_k[at + 1] = land[k, 0, b + 1]
            turn(win_v, at, land[k, 1, b], land[k, 1, b + 1])
            return c

        lax.fori_loop(0, bpc // 2, pair, 0)

    order = [nh - 1 - k for k in range(nh - 1)]
    a_copy(0).start()
    a_copy(1).start()
    for k in order[:4]:
        send_own(k)

    load_k.wait()
    load_v.wait()
    for part in range(nx):
        for slot in range(per):
            rel = vert[0, part * per + slot] - ctx * nb
            mine = (rel >= 0) & (rel < nb)
            at = jnp.minimum(jnp.maximum(rel, 0), nb - 1)
            ext[part, slot] = jnp.where(mine, win_k[own0 + at], jnp.zeros((BLK, HD), BF16))
            ext[part, per + slot] = jnp.where(mine, v_buf[at], jnp.zeros((BLK, HD), BF16))

    def xs_copy(d):
        return remote(ext.at[(x + d) % nx], rx.at[d - 1], xs_send.at[d - 1], xs_recv.at[d - 1], xpeer(d), me)

    def zs_copy(d):
        return remote(sx.at[(z + d) % nz], rz.at[d - 1], zs_send.at[d - 1], zs_recv.at[d - 1], zpeer(d), me)

    def zg_copy(d, src):
        return remote(vall.at[x, src], vall.at[x, src], zg_send.at[d - 1], zg_recv.at[d - 1], zpeer(d), me)

    def xg_copy(d, row, p):
        return remote(vall.at[row, p], vall.at[row, p], xg_send.at[d - 1, p], xg_recv.at[d - 1, p], xpeer(d), me)

    for d in range(1, nx):
        xs_copy(d).start()

    def own_turn(p, c):
        turn(win_v, own0 + 2 * p, v_buf[2 * p], v_buf[2 * p + 1])
        return c

    lax.fori_loop(0, nb // 2, own_turn, 0)

    for d in range(1, nx):
        xs_copy(d).wait_recv()
    sx[...] = ext[x]
    for d in range(1, nx):
        sx[...] = sx[...] + rx[d - 1]
    for d in range(1, nz):
        zs_copy(d).start()
    for k in order[4:6]:
        send_own(k)
    a_copy(0).wait_recv()
    a_copy(1).wait_recv()
    b_copy().start()
    for d in range(1, nz):
        zs_copy(d).wait_recv()
    piece = sx[z]
    for d in range(1, nz):
        piece = piece + rz[d - 1]
    vall[x, z] = piece
    for d in range(1, nz):
        zg_copy(d, z).start()
    for d in range(1, nx):
        xg_copy(d, x, z).start()
    for k in order[6:]:
        send_own(k)

    def take(j, c):
        k = nh - 1 - j
        own_copy(k, 0).wait_recv()
        own_copy(k, 1).wait_recv()
        fwd_copy(k).start()
        place(land1, k, nb)
        return c

    early = min(2, nh - 1)
    lax.fori_loop(0, early, take, 0)
    for d in range(1, nz):
        src = (z + nz - d) % nz
        zg_copy(d, src).wait_recv()
        for e in range(1, nx):
            xg_copy(e, x, src).start()
    b_copy().wait_recv()
    c_copy().start()
    lax.fori_loop(early, nh - 1, take, 0)

    for d in range(1, nx):
        row = (x + nx - d) % nx
        for p in range(nz):
            xg_copy(d, row, p).wait_recv()
    for part in range(nx):
        vturn[part] = vall[part, per:2 * per].reshape(per * BLK, HD).T
    load_q.wait()
    c_copy().wait_recv()
    place(land1, 0, nb)

    factor = math.log2(math.e) / math.sqrt(HD)
    nt = (((1,), (1,)), ((), ()))
    key_at = lax.broadcasted_iota(jnp.int32, (BLK, qrows), 0)
    row_at = lax.broadcasted_iota(jnp.int32, (BLK, qrows), 1) % BLK
    lanes = lax.broadcasted_iota(jnp.int32, (HD, 2 * BLK), 1)
    low = jnp.where(lanes < BLK, 1.0, 0.0).astype(BF16)
    high = jnp.where(lanes < BLK, 0.0, 1.0).astype(BF16)

    def offset(n):
        first = slash[0, 0]
        own = slash[0, n]
        return jnp.int32(0) if n == 0 else jnp.where(own == 0, first, own)

    tiles = [(g, per) for g in range(nx)] + [(nx + g, group) for g in range(ns // group)]
    starts = [sum(w for _, w in tiles[:t]) for t in range(len(tiles))]

    def scorer(r, buf, slot):
        q = q_buf[pl.ds(pl.multiple_of(r * BLK, BLK), BLK), :]
        qs = jnp.concatenate([q[:, h * HD:(h + 1) * HD] for h in range(hq)], axis=0)
        i = ctx * nb + r
        state = [jnp.full((8, qrows), NEG, F32)]

        def tile(t):
            g, width = tiles[t]
            if g < nx:
                kk = vall[g, 0:per].reshape(per * BLK, HD)
            else:
                kk = jnp.concatenate([win_k[r + own0 - offset((g - nx) * group + n)] for n in range(group)], axis=0)
            s = lax.dot_general(kk, qs, nt, preferred_element_type=F32)
            for n in range(width):
                at = starts[t] + n
                block = s[n * BLK:(n + 1) * BLK]
                if g < nx:
                    shift = jnp.where(vert[0, at] < i, 0.0, NEG)
                elif at == nv:
                    block = jnp.where(key_at > row_at, NEG, block)
                    shift = jnp.float32(0.0)
                else:
                    target = i - offset(at - nv)
                    bad = target < 0
                    for m in range(nv):
                        bad = bad | (target == vert[0, m])
                    shift = jnp.where(bad, NEG, 0.0)
                shifts[slot, at] = shift
                buf[at * BLK:(at + 1) * BLK, :] = block
                state[0] = jnp.maximum(state[0], jnp.max(block.reshape(BLK // 8, 8, qrows), axis=0) + shift)

        def done():
            tops[slot] = jnp.broadcast_to(jnp.max(state[0], axis=0, keepdims=True) * factor, (8, qrows))

        return tile, done

    def weigher(r, buf, slot):
        top = tops[slot, 0:1]
        state = [jnp.zeros((8, qrows), F32), jnp.zeros((HD, qrows), F32)]

        def tile(t):
            g, width = tiles[t]
            ws = []
            for n in range(width):
                at = starts[t] + n
                w = jnp.exp2(buf[at * BLK:(at + 1) * BLK, :] * factor - (top - shifts[slot, at]))
                state[0] = state[0] + jnp.sum(w.reshape(BLK // 8, 8, qrows), axis=0)
                ws.append(w.astype(BF16))
            w = jnp.concatenate(ws, axis=0)
            if g < nx:
                vt = vturn[g]
            else:
                pairs = []
                for n in range(0, group, 2):
                    one = r + own0 - offset((g - nx) * group + n)
                    two = r + own0 - offset((g - nx) * group + n + 1)
                    pairs.append(win_v[one] * low + win_v[two ^ 1] * high)
                vt = jnp.concatenate(pairs, axis=1)
            state[1] = state[1] + jnp.dot(vt, w, preferred_element_type=F32)

        def done():
            o = (state[1] / jnp.sum(state[0], axis=0, keepdims=True)).T.astype(BF16)
            for h in range(hq):
                stage[r // bpc, pl.ds(pl.multiple_of((r % bpc) * BLK, BLK), BLK), h * HD:(h + 1) * HD] = o[h * BLK:(h + 1) * BLK]

        return tile, done

    def both(r_next, buf_next, slot_next, r, buf, slot):
        score, score_done = scorer(r_next, buf_next, slot_next)
        weigh, weigh_done = weigher(r, buf, slot)
        for t in range(len(tiles)):
            score(t)
            weigh(t)
        score_done()
        weigh_done()

    def out_copy(ch):
        return remote(stage.at[ch], out_ref.at[:, pl.ds(pl.multiple_of(me * cols, cols), cols)], out_send.at[ch],
                      out_recv.at[me], ctx, ch)

    def out_arrival(src):
        return remote(stage.at[src], out_ref.at[:, pl.ds(pl.multiple_of(src * cols, cols), cols)], out_send.at[src],
                      out_recv.at[src], ctx, src)

    def out_local():
        return pltpu.make_async_copy(stage.at[me], out_ref.at[:, pl.ds(pl.multiple_of(me * cols, cols), cols)], loc_sem.at[3])

    last = nb - 1
    fwd_copy(nh - 1).wait_recv()
    place(land2, nh - 1, 0)
    score, score_done = scorer(last, buf_a, 0)
    for t in range(len(tiles)):
        score(t)
    score_done()

    def two_blocks(u, carry):
        odd = last - 2 * u
        both(odd - 1, buf_b, 1, odd, buf_a, 0)
        even = odd - 1
        ch = even // bpc
        ends = even % bpc == 0

        @pl.when(ends & (ch > 1))
        def _():
            fwd_copy(ch - 1).wait_recv()

        @pl.when(ends & (ch > 0))
        def _():
            place(land2, ch - 1, 0)

        both(jnp.maximum(even - 1, 0), buf_a, 0, even, buf_b, 1)

        @pl.when(ends & (ch != me))
        def _():
            out_copy(ch).start()

        @pl.when(ends & (ch == me))
        def _():
            out_local().start()

        return carry

    lax.fori_loop(0, nb // 2, two_blocks, 0)

    for k in range(1, nh):
        own_copy(k, 0).wait_send()
        own_copy(k, 1).wait_send()
        fwd_copy(k).wait_send()
    a_copy(0).wait_send()
    a_copy(1).wait_send()
    b_copy().wait_send()
    c_copy().wait_send()
    for d in range(1, nx):
        xs_copy(d).wait_send()
        for p in range(nz):
            xg_copy(d, x, p).wait_send()
    for d in range(1, nz):
        zs_copy(d).wait_send()
        zg_copy(d, z).wait_send()
    for ch in range(nh):
        @pl.when(ch != me)
        def _(ch=ch):
            out_copy(ch).wait_send()
            out_arrival(ch).wait_recv()
    out_local().wait()


def solution(mesh, nx=NX):
    nh = mesh.shape["head"]
    nctx = mesh.shape["ctx"]
    nz = nctx // nx

    def local(queries, keys, values, vertical, slash):
        tok, qcols = queries.shape
        hq = qcols // HD
        nb = tok // BLK
        nv = vertical.shape[1]
        ns = slash.shape[1]
        assert 2 * nv == nx * nz
        cfg = (nx, nz, nh, nv, ns, nb, hq)
        rows = tok // nh
        per = nv // nx
        dma = pltpu.SemaphoreType.DMA
        hbm = pl.BlockSpec(memory_space=pl.ANY)
        smem = pl.BlockSpec(memory_space=pltpu.SMEM)
        return pl.pallas_call(
            functools.partial(kernel, cfg),
            out_shape=jax.ShapeDtypeStruct((rows, nh * qcols), BF16),
            in_specs=[smem, smem, hbm, hbm, hbm],
            out_specs=hbm,
            scratch_shapes=[
                pltpu.VMEM((tok, qcols), BF16),
                pltpu.VMEM((nb, BLK, HD), BF16),
                pltpu.VMEM(((LOOK + 1) * nb, BLK, HD), BF16),
                pltpu.VMEM(((LOOK + 1) * nb, HD, 2 * BLK), BF16),
                pltpu.VMEM((nh, 2, nb // nh, BLK, HD), BF16),
                pltpu.VMEM((nh, 2, nb // nh, BLK, HD), BF16),
                pltpu.VMEM((2, nb // nh, BLK, HD), BF16),
                pltpu.VMEM((nx, nz, BLK, HD), BF16),
                pltpu.VMEM((nx - 1, nz, BLK, HD), BF16),
                pltpu.VMEM((nz, BLK, HD), BF16),
                pltpu.VMEM((nz - 1, BLK, HD), BF16),
                pltpu.VMEM((nx, nz, BLK, HD), BF16),
                pltpu.VMEM((nx, HD, per * BLK), BF16),
                pltpu.VMEM((nh, rows, qcols), BF16),
                pltpu.VMEM(((nv + ns) * BLK, hq * BLK), F32),
                pltpu.VMEM(((nv + ns) * BLK, hq * BLK), F32),
                pltpu.VMEM((2, 8, hq * BLK), F32),
                pltpu.SMEM((2, nv + ns), F32),
                dma((nh, 2)), dma((nh, 2)), dma((nh,)), dma((nh,)), dma((2,)), dma((2,)), dma((2,)), dma((2,)),
                dma((nx - 1,)), dma((nx - 1,)), dma((nz - 1,)), dma((nz - 1,)),
                dma((nz - 1,)), dma((nz - 1,)), dma((nx - 1, nz)), dma((nx - 1, nz)),
                dma((nh,)), dma((nh,)), dma((4,)),
            ],
            compiler_params=pltpu.CompilerParams(collective_id=0, has_side_effects=True, vmem_limit_bytes=56 * 1024 * 1024),
        )(vertical, slash, queries, keys.reshape(nb, BLK, HD), values.reshape(nb, BLK, HD))

    in_specs = (P("ctx", "head"), P("ctx", "head"), P("ctx", "head"), P("head", None), P("head", None))
    return jax.shard_map(local, mesh=mesh, in_specs=in_specs, out_specs=P(("ctx", "head"), None), check_vma=False)
```

time: 132 us -> 120 us (0.909)
  Pallas kernels: 128 us -> 115 us
    pallas_call x1, Pallas kernels: 128 us -> 115 us  [local(): pl.pallas_call(functools.partial(kernel, cfg), out_shape=jax.ShapeDtypeSt...]
where the time goes in v2:
time: 120 us; the launch traced here: 119 us
  Pallas kernels  115 us (96%)
  local copies, waits for them, and re-layouts  3.13 us (3%)
    pallas_call x1, Pallas kernels, local(): pl.pallas_call(functools.partial(kernel, cfg), out_shape=jax.ShapeDtypeSt...  115 us
    unnamed x1, local copies, waits for them, and re-layouts  3.13 us

profile of v2, /device:TPU:0, one launch (start us, length us, event | category | flops | bytes accessed | tf_op | source)
XLA Modules:
  0.0 118.6 jit_solution(16246213621115598018)
XLA Ops:
  0.0 115.5 %shard_map.55 = bf16[256,4096]{1,0:T(8,128)(2,1)} custom-call(s32[1,16]{1,0:T(1,128)} %vert.1, s32[1,8]{1,0:T(1,128)} %slash.1, bf16[2048,512]{1,0:T(8,128)(2,1)} %q_ref.1, bf16[32,64,128]{2,1,0:T(8,128)(2,1)} %bitcast.2, bf16[32,64,128]{2,1,0:T(8,128)(2,1)} %bitcast.3), custom_call_target="tpu_custom_call" | custom-call | tf_op jit(solution)/shard_map/pallas_call | solution.py:384
  115.5 3.1 %copy.7 = bf16[256,4096]{1,0:T(8,128)(2,1)} copy(bf16[256,4096]{1,0:T(8,128)(2,1)} %shard_map.55) | data formatting | bytes 4194304

commit v3 on v2

--- a/solution.py
+++ b/solution.py
@@ -18,8 +18,8 @@
 BF16 = jnp.bfloat16
 
 
-def kernel(cfg, vert, slash, q_ref, k_ref, v_ref, out_ref, q_buf, v_buf, win_k, win_v, land1, land2, land_a, ext, rx, sx, rz,
-           vall, vturn, stage, buf_a, buf_b, tops, shifts, own_send, own_recv, fwd_send, fwd_recv, a_send, a_recv, bc_send, bc_recv, xs_send, xs_recv,
+def kernel(cfg, vert, slash, q_ref, k_ref, v_ref, out_ref, q_buf, v_buf, win_k, win_v, land1, land2, land_a, land_r, ext, rx, sx, rz,
+           vall, vturn, stage, buf_a, buf_b, tops, shifts, own_send, own_recv, fwd_send, fwd_recv, a_send, a_recv, bc_send, bc_recv, r_send, r_recv, xs_send, xs_recv,
            zs_send, zs_recv, zg_send, zg_recv, xg_send, xg_recv, out_send, out_recv, loc_sem):
     nx, nz, nh, nv, ns, nb, hq = cfg
     nctx = nx * nz
@@ -80,6 +80,18 @@
     def fwd_copy(k):
         return remote(land1.at[k], land2.at[k], fwd_send.at[k], fwd_recv.at[k], nxt, me)
 
+    def turn_copy(k):
+        return remote(land1.at[k], land_r.at[k], fwd_send.at[k], r_recv.at[k], xpeer(1), me)
+
+    def relay_copy(k):
+        return remote(land_r.at[k], land2.at[k], r_send.at[k], fwd_recv.at[k], x * nz, me)
+
+    def relay(k):
+        @pl.when(z == nz - 1)
+        def _():
+            turn_copy(k).wait_recv()
+            relay_copy(k).start()
+
     def a_copy(part):
         ref = k_ref if part == 0 else v_ref
         return remote(ref.at[pl.ds(0, bpc)], land_a.at[part], a_send.at[part], a_recv.at[part], zpeer(nz - half), me)
@@ -112,8 +124,10 @@
     order = [nh - 1 - k for k in range(nh - 1)]
     a_copy(0).start()
     a_copy(1).start()
-    for k in order[:4]:
-        send_own(k)
+    @pl.when(z != nz - 1)
+    def _():
+        for k in order[:4]:
+            send_own(k)
 
     load_k.wait()
     load_v.wait()
@@ -153,6 +167,11 @@
         sx[...] = sx[...] + rx[d - 1]
     for d in range(1, nz):
         zs_copy(d).start()
+    @pl.when(z == nz - 1)
+    def _():
+        for k in order[:4]:
+            send_own(k)
+
     for k in order[4:6]:
         send_own(k)
     a_copy(0).wait_recv()
@@ -175,8 +194,21 @@
         k = nh - 1 - j
         own_copy(k, 0).wait_recv()
         own_copy(k, 1).wait_recv()
-        fwd_copy(k).start()
+
+        @pl.when(z != nz - 1)
+        def _():
+            fwd_copy(k).start()
+
+        @pl.when(z == nz - 1)
+        def _():
+            turn_copy(k).start()
+
         place(land1, k, nb)
+
+        @pl.when(j > 0)
+        def _():
+            relay(k + 1)
+
         return c
 
     early = min(2, nh - 1)
@@ -189,6 +221,7 @@
     b_copy().wait_recv()
     c_copy().start()
     lax.fori_loop(early, nh - 1, take, 0)
+    relay(1)
 
     for d in range(1, nx):
         row = (x + nx - d) % nx
@@ -344,6 +377,10 @@
         own_copy(k, 0).wait_send()
         own_copy(k, 1).wait_send()
         fwd_copy(k).wait_send()
+
+        @pl.when(z == nz - 1)
+        def _(k=k):
+            relay_copy(k).wait_send()
     a_copy(0).wait_send()
     a_copy(1).wait_send()
     b_copy().wait_send()
@@ -394,6 +431,7 @@
                 pltpu.VMEM((nh, 2, nb // nh, BLK, HD), BF16),
                 pltpu.VMEM((nh, 2, nb // nh, BLK, HD), BF16),
                 pltpu.VMEM((2, nb // nh, BLK, HD), BF16),
+                pltpu.VMEM((nh, 2, nb // nh, BLK, HD), BF16),
                 pltpu.VMEM((nx, nz, BLK, HD), BF16),
                 pltpu.VMEM((nx - 1, nz, BLK, HD), BF16),
                 pltpu.VMEM((nz, BLK, HD), BF16),
@@ -405,7 +443,7 @@
                 pltpu.VMEM(((nv + ns) * BLK, hq * BLK), F32),
                 pltpu.VMEM((2, 8, hq * BLK), F32),
                 pltpu.SMEM((2, nv + ns), F32),
-                dma((nh, 2)), dma((nh, 2)), dma((nh,)), dma((nh,)), dma((2,)), dma((2,)), dma((2,)), dma((2,)),
+                dma((nh, 2)), dma((nh, 2)), dma((nh,)), dma((nh,)), dma((2,)), dma((2,)), dma((2,)), dma((2,)), dma((nh,)), dma((nh,)),
                 dma((nx - 1,)), dma((nx - 1,)), dma((nz - 1,)), dma((nz - 1,)),
                 dma((nz - 1,)), dma((nz - 1,)), dma((nx - 1, nz)), dma((nx - 1, nz)),
                 dma((nh,)), dma((nh,)), dma((4,)),

time: 120 us -> 98.4 us (0.82); the launches traced: 119 us -> 98.3 us
  Pallas kernels: 115 us -> 95.2 us
    pallas_call x1, Pallas kernels: 115 us -> 95.2 us  [local(): pl.pallas_call(functools.partial(kernel, cfg), out_shape=jax.ShapeDtypeSt...]
where the time goes in v3:
time: 98.4 us; the launch traced here: 98.3 us
  Pallas kernels  95.2 us (97%)
  local copies, waits for them, and re-layouts  3.13 us (3%)
    pallas_call x1, Pallas kernels, local(): pl.pallas_call(functools.partial(kernel, cfg), out_shape=jax.ShapeDtypeSt...  95.2 us
    unnamed x1, local copies, waits for them, and re-layouts  3.13 us

profile of v3, /device:TPU:0, one launch (start us, length us, event | category | flops | bytes accessed | tf_op | source)
XLA Modules:
  0.0 98.3 jit_solution(13462223669178212212)
XLA Ops:
  0.0 95.2 %shard_map.55 = bf16[256,4096]{1,0:T(8,128)(2,1)} custom-call(s32[1,16]{1,0:T(1,128)} %vert.1, s32[1,8]{1,0:T(1,128)} %slash.1, bf16[2048,512]{1,0:T(8,128)(2,1)} %q_ref.1, bf16[32,64,128]{2,1,0:T(8,128)(2,1)} %bitcast.2, bf16[32,64,128]{2,1,0:T(8,128)(2,1)} %bitcast.3), custom_call_target="tpu_custom_call" | custom-call | tf_op jit(solution)/shard_map/pallas_call | solution.py:421
  95.2 3.1 %copy.7 = bf16[256,4096]{1,0:T(8,128)(2,1)} copy(bf16[256,4096]{1,0:T(8,128)(2,1)} %shard_map.55) | data formatting | bytes 4194304

commit v4 on v3

--- a/solution.py
+++ b/solution.py
@@ -169,11 +169,14 @@
         zs_copy(d).start()
     @pl.when(z == nz - 1)
     def _():
-        for k in order[:4]:
+        for k in order:
             send_own(k)
 
-    for k in order[4:6]:
-        send_own(k)
+    @pl.when(z != nz - 1)
+    def _():
+        for k in order[4:5]:
+            send_own(k)
+
     a_copy(0).wait_recv()
     a_copy(1).wait_recv()
     b_copy().start()
@@ -187,8 +190,11 @@
         zg_copy(d, z).start()
     for d in range(1, nx):
         xg_copy(d, x, z).start()
-    for k in order[6:]:
-        send_own(k)
+    @pl.when(z != nz - 1)
+    def _():
+        for k in order[5:]:
+            send_own(k)
+
 
     def take(j, c):
         k = nh - 1 - j
@@ -205,12 +211,13 @@
 
         place(land1, k, nb)
 
-        @pl.when(j > 0)
-        def _():
-            relay(k + 1)
+        @pl.when(j >= lag)
+        def _():
+            relay(k + lag)
 
         return c
 
+    lag = 3
     early = min(2, nh - 1)
     lax.fori_loop(0, early, take, 0)
     for d in range(1, nz):
@@ -221,7 +228,6 @@
     b_copy().wait_recv()
     c_copy().start()
     lax.fori_loop(early, nh - 1, take, 0)
-    relay(1)
 
     for d in range(1, nx):
         row = (x + nx - d) % nx
@@ -337,6 +343,7 @@
         return pltpu.make_async_copy(stage.at[me], out_ref.at[:, pl.ds(pl.multiple_of(me * cols, cols), cols)], loc_sem.at[3])
 
     last = nb - 1
+    held = max(0, nh - 1 - lag)
     fwd_copy(nh - 1).wait_recv()
     place(land2, nh - 1, 0)
     score, score_done = scorer(last, buf_a, 0)
@@ -346,6 +353,11 @@
 
     def two_blocks(u, carry):
         odd = last - 2 * u
+
+        @pl.when((u % 2 == 0) & (u >= 2) & (u // 2 <= nh - 1 - held))
+        def _():
+            relay(nh - held - u // 2)
+
         both(odd - 1, buf_b, 1, odd, buf_a, 0)
         even = odd - 1
         ch = even // bpc

time: 98.4 us -> 97.6 us (level); the launches traced: 98.3 us -> 95.9 us
  Pallas kernels: 95.2 us -> 92.8 us
    pallas_call x1, Pallas kernels: 95.2 us -> 92.8 us  [local(): pl.pallas_call(functools.partial(kernel, cfg), out_shape=jax.ShapeDtypeSt...]
where the time goes in v4:
time: 97.6 us; the launch traced here: 95.9 us
  Pallas kernels  92.8 us (95%)
  local copies, waits for them, and re-layouts  3.13 us (3%)
    pallas_call x1, Pallas kernels, local(): pl.pallas_call(functools.partial(kernel, cfg), out_shape=jax.ShapeDtypeSt...  92.8 us
    unnamed x1, local copies, waits for them, and re-layouts  3.13 us

profile of v4, /device:TPU:0, one launch (start us, length us, event | category | flops | bytes accessed | tf_op | source)
XLA Modules:
  0.0 95.9 jit_solution(4681514090573187334)
XLA Ops:
  0.0 92.8 %shard_map.55 = bf16[256,4096]{1,0:T(8,128)(2,1)} custom-call(s32[1,16]{1,0:T(1,128)} %vert.1, s32[1,8]{1,0:T(1,128)} %slash.1, bf16[2048,512]{1,0:T(8,128)(2,1)} %q_ref.1, bf16[32,64,128]{2,1,0:T(8,128)(2,1)} %bitcast.2, bf16[32,64,128]{2,1,0:T(8,128)(2,1)} %bitcast.3), custom_call_target="tpu_custom_call" | custom-call | tf_op jit(solution)/shard_map/pallas_call | solution.py:433
  92.8 3.1 %copy.7 = bf16[256,4096]{1,0:T(8,128)(2,1)} copy(bf16[256,4096]{1,0:T(8,128)(2,1)} %shard_map.55) | data formatting | bytes 4194304
